TPU v7x, 512 devices: a whole 4x8x8 slice. The times are simulated.
512 devices in a mesh: pages: 64 (over y, z_lo, core), heads: 8 (over x, z_hi).
Axes of the slice: x: 4, y: 8, z: 8 (z_hi: 2, z_lo: 4; z = z_hi * 4 + z_lo), core: 2. Of those that a mesh axis runs over, the one named last changes fastest.
Arguments:
- candidates: bfloat16 [49152, 1024], P(('pages', 'heads')), may hold values from -6 to 6
- in_weight: bfloat16 [2, 1024, 8, 512], P(None, None, 'heads'), may hold values from -0.1875 to 0.1875
- out_weight: bfloat16 [2, 8, 128, 1024], P(None, 'heads'), may hold values from -0.1875 to 0.1875
- page_cache: bfloat16 [2, 4096, 8, 2, 32, 128], P(None, 'pages', 'heads'), may hold values from -6 to 6
- page_lists: int32 [1024, 4], P('pages'), may hold values from 0 to 4095, as said below
- hist_len: int32 [1024], P('pages'), may hold values from 1 to 128
Outputs:
- hidden_out: bfloat16 [49152, 1024], P(('pages', 'heads'))
Inputs may be any that keep to these rules, and one draw needn't show every extreme that they name: `page_lists`: every page id appears in exactly one list. Page p lies on index p // 64 of pages; the requests of one index of pages list either none or exactly 2 pages that lie on any one index.
All inputs are finite; a program needn't handle non-finite values.
Results may differ from a plain program's by a relative error of at most 0.018.
Values may be sent and summed in bfloat16 or wider, within the bound.
A program may use at most 64 MiB of HBM per device.

v0:
```python
import math
import jax
import jax.numpy as jnp
from jax import lax
from jax.sharding import PartitionSpec as P

eps = 1e-05


def layer_norm(values):
    row_mean = jnp.mean(values, -1, keepdims=True)
    centred = values - row_mean
    spread = jnp.mean(centred * centred, -1, keepdims=True)
    return centred * lax.rsqrt(spread + eps)


def on_device(candidates, in_weight, out_weight, page_cache, page_lists, hist_len):
    readers = lax.axis_size("pages")
    head_group = lax.axis_size("heads")
    layers = in_weight.shape[0]
    model_width = in_weight.shape[1]
    heads_here = in_weight.shape[2]
    head_dim = out_weight.shape[2]
    pages_here = page_cache.shape[1]
    page_len = page_cache.shape[4]
    requests, max_pages = page_lists.shape
    slot_count = requests * max_pages
    capacity = 2 * slot_count // readers
    shard_rows = candidates.shape[0]
    cand_rows = shard_rows * head_group
    per_request = cand_rows // requests
    score_scale = 1.0 / math.sqrt(head_dim)
    flat_ids = page_lists.reshape(slot_count)
    slot_owner = flat_ids // pages_here
    local_ids = flat_ids % pages_here
    slot_order = jnp.arange(slot_count)
    earlier_same = (slot_owner[None, :] == slot_owner[:, None]) & (
        slot_order[None, :] < slot_order[:, None]
    )
    slot_rank = jnp.sum(earlier_same.astype(jnp.int32), axis=1)
    places = slot_owner * capacity + slot_rank
    divisors = (hist_len + 1).astype(jnp.float32)
    cand_divisors = jnp.repeat(divisors, per_request)
    slot_targets = jnp.arange(readers * capacity)
    matches = places[None, :] == slot_targets[:, None]
    filled = jnp.any(matches, axis=1)
    inverse = jnp.sum(jnp.where(matches, slot_order[None, :], 0), axis=1)
    asked_request = inverse // max_pages
    page_of_slot = slot_order % max_pages
    valid_tokens = jnp.clip(jnp.repeat(hist_len, max_pages) - page_of_slot * page_len, 0, page_len)
    slot_meta = jnp.stack(
        [
            jnp.take(local_ids, inverse),
            jnp.take(valid_tokens, inverse),
            jnp.take(hist_len, asked_request),
        ],
        axis=-1,
    )
    slot_meta = jnp.where(filled[:, None], slot_meta, 0).reshape(readers, capacity, 3)
    hidden_rows = candidates
    for layer_index in range(layers):
        weights_in = in_weight[layer_index].reshape(model_width, heads_here * 4 * head_dim)
        ready = layer_norm(
            lax.all_gather(hidden_rows, "heads", axis=0, tiled=True).astype(jnp.float32)
        ).astype(jnp.bfloat16)
        projected = jax.nn.silu(jnp.dot(ready, weights_in, preferred_element_type=jnp.float32))
        projected = projected.reshape(cand_rows, heads_here, 4 * head_dim)
        gate_part = projected[:, :, :head_dim]
        value_part = projected[:, :, head_dim : 2 * head_dim].astype(jnp.bfloat16)
        query_part = projected[:, :, 2 * head_dim : 3 * head_dim].astype(jnp.bfloat16)
        key_part = projected[:, :, 3 * head_dim :].astype(jnp.bfloat16)
        queries = query_part.reshape(requests, per_request, heads_here, head_dim)
        sent_queries = jnp.take(queries, asked_request, axis=0)
        sent_queries = jnp.where(
            filled[:, None, None, None], sent_queries, jnp.zeros((), jnp.bfloat16)
        )
        sent_queries = sent_queries.reshape(readers, capacity, per_request, heads_here, head_dim)
        got_queries, got_meta = (
            lax.all_to_all(sent_queries, "pages", split_axis=0, concat_axis=0, tiled=True),
            lax.all_to_all(slot_meta, "pages", split_axis=0, concat_axis=0, tiled=True),
        )
        page_rows = jnp.take(
            page_cache[layer_index], got_meta[:, :, 0].reshape(readers * capacity), axis=0
        )
        page_rows = page_rows.reshape(readers, capacity, heads_here, 2, page_len, head_dim)
        scores = (
            jnp.einsum(
                "ncqhd,nchtd->nchqt",
                got_queries,
                page_rows[:, :, :, 0],
                preferred_element_type=jnp.float32,
            )
            * score_scale
        )
        keep_mask = jnp.arange(page_len)[None, None, :] < got_meta[:, :, 1][:, :, None]
        owner_divisors = (got_meta[:, :, 2] + 1).astype(jnp.float32)
        weights = (
            jnp.where(keep_mask[:, :, None, None, :], jax.nn.silu(scores), 0.0)
            / owner_divisors[:, :, None, None, None]
        )
        weights = weights.astype(jnp.bfloat16)
        partial_out = jnp.einsum(
            "nchqt,nchtd->ncqhd", weights, page_rows[:, :, :, 1], preferred_element_type=jnp.float32
        )
        returned = lax.all_to_all(
            partial_out.astype(jnp.bfloat16), "pages", split_axis=0, concat_axis=0, tiled=True
        ).astype(partial_out.dtype)
        returned_rows = jnp.take(
            returned.reshape(readers * capacity, per_request, heads_here, head_dim), places, axis=0
        )
        attended_hist = jnp.sum(
            returned_rows.reshape(requests, max_pages, per_request, heads_here, head_dim), axis=1
        )
        attended = attended_hist.reshape(cand_rows, heads_here, head_dim)
        self_score = (
            jnp.sum(query_part.astype(jnp.float32) * key_part.astype(jnp.float32), -1) * score_scale
        )
        self_weight = (jax.nn.silu(self_score) / cand_divisors[:, None]).astype(jnp.bfloat16)
        attended = attended + self_weight.astype(jnp.float32)[:, :, None] * value_part.astype(
            jnp.float32
        )
        gated_rows = (
            (layer_norm(attended) * gate_part)
            .astype(jnp.bfloat16)
            .reshape(cand_rows, heads_here * head_dim)
        )
        weights_out = out_weight[layer_index].reshape(heads_here * head_dim, model_width)
        summed = lax.psum_scatter(
            jnp.dot(gated_rows, weights_out, preferred_element_type=jnp.float32).astype(
                jnp.bfloat16
            ),
            "heads",
            scatter_dimension=0,
            tiled=True,
        ).astype(jnp.float32)
        hidden_rows = (hidden_rows.astype(jnp.float32) + summed).astype(jnp.bfloat16)
    return hidden_rows


def solution(mesh):
    in_specs = (
        P(("pages", "heads"), None),
        P(None, None, "heads", None),
        P(None, "heads", None, None),
        P(None, "pages", "heads", None, None, None),
        P("pages", None),
        P("pages"),
    )
    out_specs = P(("pages", "heads"), None)
    return jax.shard_map(
        on_device, mesh=mesh, in_specs=in_specs, out_specs=out_specs, check_vma=False
    )
```

profile of v0, /device:TPU:8, one launch (start us, length us, event | category | flops | bytes accessed | tf_op | source)
XLA Modules:
  0.0 597.3 jit_solution(8234759997289166943)
XLA Ops:
  6.5 0.7 all-gather.3.cloned.1.call-update
  7.3 0.8 copy.53
  8.1 0.7 broadcast_in_dim.133
  8.9 0.2 convert_reduce_fusion.2
  9.4 1.2 gather_fusion
  10.6 1.2 gather_fusion.1
  11.9 2.0 fusion.69
  13.8 10.1 %broadcast_select_fusion.1 = (s32[128]{0:T(128)S(1)}, s32[128]{0:T(128)S(1)}, s32[128]{0:T(128)S(1)}) fusion(s32[128]{0:T(128)S(1)} %gather_fusion, s32[128]{0:T(128)S(1)} %select_reduce_fusion, s32[128]{0:T(128)S(1)} %gather_fusion.1, s32[]{:T(128)} %bitcast.25, s32[]{:T(128)} %bitcast.24, s32[]{:T(128)} %bitcast.23, s32[]{:T(128)} %bitcast.22, ...), kind=kLoop, calls=%fused_computation.158 | loop fusion | flops 7168 | bytes 3136 | tf_op jit(solution)/shard_map/jit(_take)/select_n | solution.py:53
  24.2 0.2 stack.10
  24.8 0.2 broadcast_in_dim.129
  25.1 0.7 copy.62
  25.8 13.5 %all-to-all-start = ((s32[64,2,3]{2,1,0:T(2,128)}), s32[64,2,3]{2,1,0:T(2,128)S(1)}, u32[]{:S(2)}, u32[]{:S(2)}) async-start(s32[64,2,3]{2,1,0:T(2,128)} %copy.62), calls=%async_computation | async-start | bytes 131072 | tf_op jit(solution)/shard_map/all_to_all | solution.py:80
  39.4 50.6 %all-gather.3.cloned.1.call-done = bf16[768,1024]{1,0:T(8,128)(2,1)} async-done(((bf16[96,1024]{1,0:T(8,128)(2,1)}), bf16[768,1024]{1,0:T(8,128)(2,1)}) %all-gather.3.cloned.1.call-update) | async-done | bytes 1572880 | tf_op jit(solution)/shard_map/all_gather | solution.py:64
  90.1 1.8 convert_reduce_fusion.1
  91.9 0.6 fusion.6
  92.5 3.7 fusion.70
  96.2 0.9 gather_fusion.3
  97.1 1.6 fusion.15
  98.7 8.5 %all-to-all-start.1 = ((bf16[64,2,48,1,128]{4,2,1,3,0:T(8,128)(2,1)}), bf16[64,2,48,1,128]{4,2,1,3,0:T(8,128)(2,1)}, u32[]{:S(2)}, u32[]{:S(2)}) async-start(bf16[64,2,48,1,128]{4,2,1,3,0:T(8,128)(2,1)} %bitcast.38), calls=%async_computation.1 | async-start | bytes 3145728 | tf_op jit(solution)/shard_map/all_to_all | solution.py:79
  107.2 2.0 slice_bitcast_fusion.8
  109.2 1.3 fusion.68
  110.6 2.1 gather_fusion.2
  112.7 2.2 gather_fusion.5
  114.9 2.7 bitcast_select_fusion
  117.6 1.7 copy.63
  119.7 0.1 iota_compare_fusion
  119.8 26.4 %all-to-all-done.1 = bf16[64,2,48,1,128]{4,2,1,3,0:T(8,128)(2,1)} async-done(((bf16[64,2,48,1,128]{4,2,1,3,0:T(8,128)(2,1)}), bf16[64,2,48,1,128]{4,2,1,3,0:T(8,128)(2,1)}, u32[]{:S(2)}, u32[]{:S(2)}) %all-to-all-start.1) | async-done | bytes 1572896 | tf_op jit(solution)/shard_map/all_to_all | solution.py:79
  146.3 4.0 fusion.20
  150.3 6.9 %all-to-all-start.2 = ((bf16[64,2,48,1,128]{4,2,1,3,0:T(8,128)(2,1)}), bf16[64,2,48,1,128]{4,2,1,3,0:T(8,128)(2,1)}, u32[]{:S(2)}, u32[]{:S(2)}) async-start(bf16[64,2,48,1,128]{4,2,1,3,0:T(8,128)(2,1)} %fusion.20), calls=%async_computation.2 | async-start | bytes 3145728 | tf_op jit(solution)/shard_map/all_to_all | solution.py:105
  157.2 0.2 reduce-scatter.3.cloned.1.call-start
  157.6 0.2 multiply_reduce_fusion.3
  157.8 38.5 %all-to-all-done.2 = bf16[64,2,48,1,128]{4,2,1,3,0:T(8,128)(2,1)} async-done(((bf16[64,2,48,1,128]{4,2,1,3,0:T(8,128)(2,1)}), bf16[64,2,48,1,128]{4,2,1,3,0:T(8,128)(2,1)}, u32[]{:S(2)}, u32[]{:S(2)}) %all-to-all-start.2) | async-done | bytes 1572896 | tf_op jit(solution)/shard_map/all_to_all | solution.py:105
  196.2 3.3 bitcast_convert_fusion.1
  199.6 3.7 gather_fusion.4
  203.3 2.8 bitcast_select_fusion.4
  206.1 1.5 reduce_sum.136
  207.6 0.3 fusion.67
  207.9 0.3 multiply_reduce_fusion.2
  208.2 0.4 copy-done.4
  208.6 2.8 convolution_convert_fusion.3
  211.5 92.5 %reduce-scatter.3.cloned.1.call-done = bf16[96,1024]{1,0:T(8,128)(2,1)} async-done(((bf16[768,1024]{1,0:T(8,128)(2,1)}), bf16[96,1024]{1,0:T(8,128)(2,1)}) %reduce-scatter.3.cloned.1.call-update) | async-done | bytes 196624 | tf_op jit(solution)/shard_map/reduce_scatter | solution.py:128
  304.1 1.7 add_convert_fusion.1
  305.8 71.9 %all-gather.5.cloned.1.call-done = bf16[768,1024]{1,0:T(8,128)(2,1)} async-done(((bf16[96,1024]{1,0:T(8,128)(2,1)}), bf16[768,1024]{1,0:T(8,128)(2,1)}) %all-gather.5.cloned.1.call-update) | async-done | bytes 1572880 | tf_op jit(solution)/shard_map/all_gather | solution.py:64
  377.7 1.8 convert_reduce_fusion
  379.6 0.6 fusion.4
  380.1 3.6 fusion.71
  383.8 1.9 gather_fusion.6
  385.7 2.7 fusion.13
  388.4 8.5 %all-to-all-start.3 = ((bf16[64,2,48,1,128]{4,2,1,3,0:T(8,128)(2,1)}), bf16[64,2,48,1,128]{4,2,1,3,0:T(8,128)(2,1)}, u32[]{:S(2)}, u32[]{:S(2)}) async-start(bf16[64,2,48,1,128]{4,2,1,3,0:T(8,128)(2,1)} %bitcast.191), calls=%async_computation.4 | async-start | bytes 3145728 | tf_op jit(solution)/shard_map/all_to_all | solution.py:79
  396.9 1.7 copy.69
  398.7 37.3 %all-to-all-done.3 = bf16[64,2,48,1,128]{4,2,1,3,0:T(8,128)(2,1)} async-done(((bf16[64,2,48,1,128]{4,2,1,3,0:T(8,128)(2,1)}), bf16[64,2,48,1,128]{4,2,1,3,0:T(8,128)(2,1)}, u32[]{:S(2)}, u32[]{:S(2)}) %all-to-all-start.3) | async-done | bytes 1572896 | tf_op jit(solution)/shard_map/all_to_all | solution.py:79
  436.0 4.0 fusion.21
  440.0 6.6 %all-to-all-start.4 = ((bf16[64,2,48,1,128]{4,2,1,3,0:T(8,128)(2,1)}), bf16[64,2,48,1,128]{4,2,1,3,0:T(8,128)(2,1)S(1)}, u32[]{:S(2)}, u32[]{:S(2)}) async-start(bf16[64,2,48,1,128]{4,2,1,3,0:T(8,128)(2,1)} %fusion.21), calls=%async_computation.5 | async-start | bytes 3145728 | tf_op jit(solution)/shard_map/all_to_all | solution.py:105
  446.7 0.2 multiply_reduce_fusion.1
  446.9 38.9 %all-to-all-done.4 = bf16[64,2,48,1,128]{4,2,1,3,0:T(8,128)(2,1)S(1)} async-done(((bf16[64,2,48,1,128]{4,2,1,3,0:T(8,128)(2,1)}), bf16[64,2,48,1,128]{4,2,1,3,0:T(8,128)(2,1)S(1)}, u32[]{:S(2)}, u32[]{:S(2)}) %all-to-all-start.4) | async-done | bytes 1572896 | tf_op jit(solution)/shard_map/all_to_all | solution.py:105
  485.8 2.0 bitcast_convert_fusion
  487.8 2.5 gather_fusion.7
  490.3 1.3 bitcast_select_fusion.2
  491.6 1.6 reduce_sum.142
  493.2 0.3 fusion.66
  493.5 0.3 multiply_reduce_fusion
  493.9 2.8 convolution_convert_fusion.2
  496.7 92.4 %reduce-scatter.5.cloned.1.call-done = bf16[96,1024]{1,0:T(8,128)(2,1)} async-done(((bf16[768,1024]{1,0:T(8,128)(2,1)}), bf16[96,1024]{1,0:T(8,128)(2,1)}) %reduce-scatter.5.cloned.1.call-update) | async-done | bytes 196624 | tf_op jit(solution)/shard_map/reduce_scatter | solution.py:128
  589.1 1.7 add_convert_fusion
  (67 shorter events, 2.4 us)
Async XLA Ops:
  6.5 83.5 %all-gather.3.cloned.1.call-start = ((), (), s32[]{:S(2)}) async-start(), calls=%async_computation.7 | async-start | bytes 1769472 | tf_op jit(solution)/shard_map/all_gather | solution.py:64
  25.8 72.8 %all-to-all-start = ((s32[64,2,3]{2,1,0:T(2,128)}), s32[64,2,3]{2,1,0:T(2,128)S(1)}, u32[]{:S(2)}, u32[]{:S(2)}) async-start(s32[64,2,3]{2,1,0:T(2,128)} %copy.62), calls=%async_computation | async-start | bytes 131072 | tf_op jit(solution)/shard_map/all_to_all | solution.py:80
  90.1 1.9 copy-start
  98.7 47.6 %all-to-all-start.1 = ((bf16[64,2,48,1,128]{4,2,1,3,0:T(8,128)(2,1)}), bf16[64,2,48,1,128]{4,2,1,3,0:T(8,128)(2,1)}, u32[]{:S(2)}, u32[]{:S(2)}) async-start(bf16[64,2,48,1,128]{4,2,1,3,0:T(8,128)(2,1)} %bitcast.38), calls=%async_computation.1 | async-start | bytes 3145728 | tf_op jit(solution)/shard_map/all_to_all | solution.py:79
  150.3 7.1 %copy-start.6 = (s32[16]{0:T(128)S(1)}, s32[16]{0:T(128)}, u32[]{:S(2)}) copy-start(s32[16]{0:T(128)} %param.19) | copy-start | bytes 196
  150.3 46.0 %all-to-all-start.2 = ((bf16[64,2,48,1,128]{4,2,1,3,0:T(8,128)(2,1)}), bf16[64,2,48,1,128]{4,2,1,3,0:T(8,128)(2,1)}, u32[]{:S(2)}, u32[]{:S(2)}) async-start(bf16[64,2,48,1,128]{4,2,1,3,0:T(8,128)(2,1)} %fusion.20), calls=%async_computation.2 | async-start | bytes 3145728 | tf_op jit(solution)/shard_map/all_to_all | solution.py:105
  157.2 146.9 %reduce-scatter.3.cloned.1.call-start = ((), (), s32[]{:S(2)}) async-start(), calls=%async_computation.8 | async-start | bytes 1769472 | tf_op jit(solution)/shard_map/reduce_scatter | solution.py:128
  207.6 1.0 copy-start.4
  208.6 95.4 %copy-start.3 = (bf16[96,1024]{1,0:T(8,128)(2,1)S(1)}, bf16[96,1024]{1,0:T(8,128)(2,1)}, u32[]{:S(2)}) copy-start(bf16[96,1024]{1,0:T(8,128)(2,1)} %param.14) | copy-start | bytes 589828
  211.5 166.2 %all-gather.5.cloned.1.call-start = ((), (), s32[]{:S(2)}) async-start(), calls=%async_computation.9 | async-start | bytes 1769472 | tf_op jit(solution)/shard_map/all_gather | solution.py:64
  377.7 1.9 copy-start.1
  388.4 47.6 %all-to-all-start.3 = ((bf16[64,2,48,1,128]{4,2,1,3,0:T(8,128)(2,1)}), bf16[64,2,48,1,128]{4,2,1,3,0:T(8,128)(2,1)}, u32[]{:S(2)}, u32[]{:S(2)}) async-start(bf16[64,2,48,1,128]{4,2,1,3,0:T(8,128)(2,1)} %bitcast.191), calls=%async_computation.4 | async-start | bytes 3145728 | tf_op jit(solution)/shard_map/all_to_all | solution.py:79
  440.0 45.7 %all-to-all-start.4 = ((bf16[64,2,48,1,128]{4,2,1,3,0:T(8,128)(2,1)}), bf16[64,2,48,1,128]{4,2,1,3,0:T(8,128)(2,1)S(1)}, u32[]{:S(2)}, u32[]{:S(2)}) async-start(bf16[64,2,48,1,128]{4,2,1,3,0:T(8,128)(2,1)} %fusion.21), calls=%async_computation.5 | async-start | bytes 3145728 | tf_op jit(solution)/shard_map/all_to_all | solution.py:105
  446.6 142.5 %reduce-scatter.5.cloned.1.call-start = ((), (), s32[]{:S(2)}) async-start(), calls=%async_computation.10 | async-start | bytes 1769472 | tf_op jit(solution)/shard_map/reduce_scatter | solution.py:128
  491.6 2.2 copy-start.5
  493.9 95.2 %copy-start.2 = (bf16[96,1024]{1,0:T(8,128)(2,1)S(1)}, bf16[96,1024]{1,0:T(8,128)(2,1)}, u32[]{:S(2)}) copy-start(bf16[96,1024]{1,0:T(8,128)(2,1)} %add_convert_fusion.1) | copy-start | bytes 589828
Sparse Core Ops, SparseCore 0:
  10.5 79.5 all-gather.2
  211.6 92.4 reduce-scatter.2
  307.3 70.3 all-gather.4
  496.8 92.2 reduce-scatter.4
where the time goes:
time: 599 us; the launch traced here: 597 us
  waiting for transfers between devices  449 us (75%)
  starting transfers between devices  44.3 us (7%)
  other arithmetic  39.9 us (7%)
  local copies, waits for them, and re-layouts  29.2 us (5%)
  matrix products  20.9 us (3%)
  between operations  13.5 us (2%)
    reduce_scatter x2, waiting for transfers between devices, on_device(): lax.psum_scatter(jnp.dot(gated_rows, weights_out, preferred_element_type=...  185 us
    all_gather x2, waiting for transfers between devices, on_device(): lax.all_gather(hidden_rows, 'heads', axis=0, tiled=True).astype(jnp.float32)  123 us
    all_to_all x2, waiting for transfers between devices, on_device(): lax.all_to_all(partial_out.astype(jnp.bfloat16), 'pages', split_axis=0, c...  77.4 us
    all_to_all x2, waiting for transfers between devices, on_device(): lax.all_to_all(sent_queries, 'pages', split_axis=0, concat_axis=0, tiled=...  63.8 us
    all_to_all x2, starting transfers between devices, on_device(): lax.all_to_all(sent_queries, 'pages', split_axis=0, concat_axis=0, tiled=...  17 us
    all_to_all x1, starting transfers between devices, on_device(): lax.all_to_all(slot_meta, 'pages', split_axis=0, concat_axis=0, tiled=True)  13.5 us
    all_to_all x2, starting transfers between devices, on_device(): lax.all_to_all(partial_out.astype(jnp.bfloat16), 'pages', split_axis=0, c...  13.5 us
  transfers between devices with their start and end apart: 9, of which 8 were waited for; matrix products, arithmetic and copies ran while one was open for 7% of the time, Pallas kernels for 0%

commit v1 on v0

--- a/solution.py
+++ b/solution.py
@@ -61,7 +61,10 @@
     for layer_index in range(layers):
         weights_in = in_weight[layer_index].reshape(model_width, heads_here * 4 * head_dim)
         ready = layer_norm(
-            lax.all_gather(hidden_rows, "heads", axis=0, tiled=True).astype(jnp.float32)
+            jnp.concatenate(
+                lax.all_to_all(jnp.stack([hidden_rows] * lax.axis_size("heads")), "heads", 0, 0),
+                axis=0,
+            ).astype(jnp.float32)
         ).astype(jnp.bfloat16)
         projected = jax.nn.silu(jnp.dot(ready, weights_in, preferred_element_type=jnp.float32))
         projected = projected.reshape(cand_rows, heads_here, 4 * head_dim)

time: 599 us -> 550 us (0.918)
  waiting for transfers between devices: 449 us -> 334 us
  starting transfers between devices: 44.3 us -> 88.4 us
  blocking collectives: 0 us -> 26.8 us
    all_gather x2 -> x0, waiting for transfers between devices: 123 us -> none  [on_device(): lax.all_gather(hidden_rows, 'heads', axis=0, tiled=True).astype(jnp.float32)]
    all_to_all x0 -> x1, blocking collectives: none -> 26.8 us  [on_device(): lax.all_to_all(jnp.stack([hidden_rows] * lax.axis_size('heads')), 'heads'...]
    all_to_all x2, starting transfers between devices: 17 us -> 35.2 us  [on_device(): lax.all_to_all(sent_queries, 'pages', split_axis=0, concat_axis=0, tiled=...]
    all_to_all x1, starting transfers between devices: 13.5 us -> 26.5 us  [on_device(): lax.all_to_all(slot_meta, 'pages', split_axis=0, concat_axis=0, tiled=True)]
    all_to_all x0 -> x1, starting transfers between devices: none -> 12.9 us  [on_device(): lax.all_to_all(jnp.stack([hidden_rows] * lax.axis_size('heads')), 'heads'...]
    all_to_all x0 -> x1, waiting for transfers between devices: none -> 9.39 us  [on_device(): lax.all_to_all(jnp.stack([hidden_rows] * lax.axis_size('heads')), 'heads'...]
  transfers between devices with their start and end apart: 9 -> 8, of which waited for: 8 -> 8; matrix products, arithmetic and copies ran while one was open for 7% -> 7% of each run, Pallas kernels for 0% -> 0%
where the time goes in v1:
time: 550 us; the launch traced here: 548 us
  waiting for transfers between devices  334 us (61%)
  starting transfers between devices  88.4 us (16%)
  other arithmetic  36.5 us (7%)
  local copies, waits for them, and re-layouts  30.6 us (6%)
  blocking collectives  26.8 us (5%)
  matrix products  18.3 us (3%)
  between operations  13.9 us (3%)
    reduce_scatter x2, waiting for transfers between devices, on_device(): lax.psum_scatter(jnp.dot(gated_rows, weights_out, preferred_element_type=...  181 us
    all_to_all x2, waiting for transfers between devices, on_device(): lax.all_to_all(partial_out.astype(jnp.bfloat16), 'pages', split_axis=0, c...  77.3 us
    all_to_all x2, waiting for transfers between devices, on_device(): lax.all_to_all(sent_queries, 'pages', split_axis=0, concat_axis=0, tiled=...  63.8 us
    all_to_all x2, starting transfers between devices, on_device(): lax.all_to_all(sent_queries, 'pages', split_axis=0, concat_axis=0, tiled=...  35.2 us
    all_to_all x1, blocking collectives, on_device(): lax.all_to_all(jnp.stack([hidden_rows] * lax.axis_size('heads')), 'heads'...  26.8 us
    all_to_all x1, starting transfers between devices, on_device(): lax.all_to_all(slot_meta, 'pages', split_axis=0, concat_axis=0, tiled=True)  26.5 us
    all_to_all x2, starting transfers between devices, on_device(): lax.all_to_all(partial_out.astype(jnp.bfloat16), 'pages', split_axis=0, c...  13.5 us
    all_to_all x1, starting transfers between devices, on_device(): lax.all_to_all(jnp.stack([hidden_rows] * lax.axis_size('heads')), 'heads'...  12.9 us
  transfers between devices with their start and end apart: 8, of which 8 were waited for; matrix products, arithmetic and copies ran while one was open for 7% of the time, Pallas kernels for 0%

profile of v1, /device:TPU:8, one launch (start us, length us, event | category | flops | bytes accessed | tf_op | source)
XLA Modules:
  0.0 548.4 jit_solution(3523454597380380697)
XLA Ops:
  6.5 2.3 stack.13
  8.8 12.9 %all-to-all-start.1 = ((bf16[8,96,1024]{2,1,0:T(8,128)(2,1)}), bf16[8,96,1024]{2,1,0:T(8,128)(2,1)S(1)}, u32[]{:S(2)}, u32[]{:S(2)}) async-start(bf16[8,96,1024]{2,1,0:T(8,128)(2,1)} %stack.13), calls=%async_computation.1 | async-start | bytes 3145728 | tf_op jit(solution)/shard_map/all_to_all | solution.py:65
  22.5 1.2 gather_fusion
  23.8 1.2 gather_fusion.1
  25.0 0.7 fusion.59
  25.7 10.1 %broadcast_select_fusion.1 = (s32[128]{0:T(128)S(1)}, s32[128]{0:T(128)S(1)}, s32[128]{0:T(128)S(1)}) fusion(s32[128]{0:T(128)S(1)} %gather_fusion, s32[128]{0:T(128)S(1)} %select_reduce_fusion, s32[128]{0:T(128)S(1)} %gather_fusion.1, s32[]{:T(128)} %bitcast.25, s32[]{:T(128)} %bitcast.24, s32[]{:T(128)} %bitcast.23, s32[]{:T(128)} %bitcast.22, ...), kind=kLoop, calls=%fused_computation.154 | loop fusion | flops 7168 | bytes 3136 | tf_op jit(solution)/shard_map/jit(_take)/select_n | solution.py:53
  37.0 0.7 copy.62
  37.8 9.4 %all-to-all-done.1 = bf16[8,96,1024]{2,1,0:T(8,128)(2,1)S(1)} async-done(((bf16[8,96,1024]{2,1,0:T(8,128)(2,1)}), bf16[8,96,1024]{2,1,0:T(8,128)(2,1)S(1)}, u32[]{:S(2)}, u32[]{:S(2)}) %all-to-all-start.1) | async-done | bytes 1572896 | tf_op jit(solution)/shard_map/all_to_all | solution.py:65
  47.1 26.5 %all-to-all-start = ((s32[64,2,3]{2,1,0:T(2,128)}), s32[64,2,3]{2,1,0:T(2,128)S(1)}, u32[]{:S(2)}, u32[]{:S(2)}) async-start(s32[64,2,3]{2,1,0:T(2,128)} %copy.62), calls=%async_computation | async-start | bytes 131072 | tf_op jit(solution)/shard_map/all_to_all | solution.py:83
  73.7 0.3 convert_reduce_fusion.1
  74.0 0.6 fusion.6
  74.6 0.4 fusion.7
  75.0 1.1 copy-done.6
  76.2 2.4 fusion.60
  78.6 0.9 gather_fusion.3
  79.4 1.6 fusion.11
  81.1 1.9 all-to-all-done
  83.0 8.8 %all-to-all-start.2 = ((bf16[64,2,48,1,128]{4,2,1,3,0:T(8,128)(2,1)}), bf16[64,2,48,1,128]{4,2,1,3,0:T(8,128)(2,1)}, u32[]{:S(2)}, u32[]{:S(2)}) async-start(bf16[64,2,48,1,128]{4,2,1,3,0:T(8,128)(2,1)} %bitcast.39), calls=%async_computation.2 | async-start | bytes 3145728 | tf_op jit(solution)/shard_map/all_to_all | solution.py:82
  91.8 2.0 slice_bitcast_fusion.8
  93.8 1.3 fusion.58
  95.3 2.1 gather_fusion.2
  97.4 2.2 gather_fusion.5
  99.6 2.7 bitcast_select_fusion
  102.2 1.7 copy.63
  104.5 26.4 %all-to-all-done.2 = bf16[64,2,48,1,128]{4,2,1,3,0:T(8,128)(2,1)} async-done(((bf16[64,2,48,1,128]{4,2,1,3,0:T(8,128)(2,1)}), bf16[64,2,48,1,128]{4,2,1,3,0:T(8,128)(2,1)}, u32[]{:S(2)}, u32[]{:S(2)}) %all-to-all-start.2) | async-done | bytes 1572896 | tf_op jit(solution)/shard_map/all_to_all | solution.py:82
  130.9 4.0 fusion.12
  134.9 6.8 %all-to-all-start.3 = ((bf16[64,2,48,1,128]{4,2,1,3,0:T(8,128)(2,1)}), bf16[64,2,48,1,128]{4,2,1,3,0:T(8,128)(2,1)}, u32[]{:S(2)}, u32[]{:S(2)}) async-start(bf16[64,2,48,1,128]{4,2,1,3,0:T(8,128)(2,1)} %fusion.12), calls=%async_computation.3 | async-start | bytes 3145728 | tf_op jit(solution)/shard_map/all_to_all | solution.py:108
  141.7 0.2 reduce-scatter.3.cloned.1.call-start
  142.1 0.2 multiply_reduce_fusion.3
  142.3 38.5 %all-to-all-done.3 = bf16[64,2,48,1,128]{4,2,1,3,0:T(8,128)(2,1)} async-done(((bf16[64,2,48,1,128]{4,2,1,3,0:T(8,128)(2,1)}), bf16[64,2,48,1,128]{4,2,1,3,0:T(8,128)(2,1)}, u32[]{:S(2)}, u32[]{:S(2)}) %all-to-all-start.3) | async-done | bytes 1572896 | tf_op jit(solution)/shard_map/all_to_all | solution.py:108
  180.8 3.3 bitcast_convert_fusion.1
  184.1 3.7 gather_fusion.4
  187.8 2.8 bitcast_select_fusion.4
  190.6 1.5 reduce_sum.136
  192.1 0.3 fusion.57
  192.4 0.3 multiply_reduce_fusion.2
  192.7 0.4 copy-done.2
  193.2 2.8 convolution_convert_fusion.3
  196.0 91.0 %reduce-scatter.3.cloned.1.call-done = bf16[96,1024]{1,0:T(8,128)(2,1)} async-done(((bf16[768,1024]{1,0:T(8,128)(2,1)}), bf16[96,1024]{1,0:T(8,128)(2,1)}) %reduce-scatter.3.cloned.1.call-update) | async-done | bytes 196624 | tf_op jit(solution)/shard_map/reduce_scatter | solution.py:131
  287.0 1.0 add_convert_fusion.1
  288.0 0.2 stack.14
  288.2 26.8 %all_to_all.36 = bf16[8,96,1024]{2,1,0:T(8,128)(2,1)S(1)} all-to-all(bf16[8,96,1024]{2,1,0:T(8,128)(2,1)S(1)} %stack.14), channel_id=1, replica_groups=mesh['pages'=64,'heads'=8] {'heads'}, dimensions={0} | all-to-all | bytes 3145728 | tf_op jit(solution)/shard_map/all_to_all | solution.py:65
  315.0 0.3 convert_reduce_fusion
  315.3 0.6 fusion.4
  315.9 0.4 fusion.5
  316.3 1.1 copy-done.7
  317.5 2.3 fusion.61
  319.8 2.0 gather_fusion.6
  321.8 2.8 fusion.9
  324.6 26.4 %all-to-all-start.5 = ((bf16[64,2,48,1,128]{4,2,1,3,0:T(8,128)(2,1)}), bf16[64,2,48,1,128]{4,2,1,3,0:T(8,128)(2,1)}, u32[]{:S(2)}, u32[]{:S(2)}) async-start(bf16[64,2,48,1,128]{4,2,1,3,0:T(8,128)(2,1)} %bitcast.195), calls=%async_computation.6 | async-start | bytes 3145728 | tf_op jit(solution)/shard_map/all_to_all | solution.py:82
  351.0 1.7 copy.69
  352.7 37.3 %all-to-all-done.5 = bf16[64,2,48,1,128]{4,2,1,3,0:T(8,128)(2,1)} async-done(((bf16[64,2,48,1,128]{4,2,1,3,0:T(8,128)(2,1)}), bf16[64,2,48,1,128]{4,2,1,3,0:T(8,128)(2,1)}, u32[]{:S(2)}, u32[]{:S(2)}) %all-to-all-start.5) | async-done | bytes 1572896 | tf_op jit(solution)/shard_map/all_to_all | solution.py:82
  390.1 4.0 fusion.13
  394.1 6.8 %all-to-all-start.6 = ((bf16[64,2,48,1,128]{4,2,1,3,0:T(8,128)(2,1)}), bf16[64,2,48,1,128]{4,2,1,3,0:T(8,128)(2,1)}, u32[]{:S(2)}, u32[]{:S(2)}) async-start(bf16[64,2,48,1,128]{4,2,1,3,0:T(8,128)(2,1)} %fusion.13), calls=%async_computation.7 | async-start | bytes 3145728 | tf_op jit(solution)/shard_map/all_to_all | solution.py:108
  400.9 0.2 multiply_reduce_fusion.1
  401.1 38.8 %all-to-all-done.6 = bf16[64,2,48,1,128]{4,2,1,3,0:T(8,128)(2,1)} async-done(((bf16[64,2,48,1,128]{4,2,1,3,0:T(8,128)(2,1)}), bf16[64,2,48,1,128]{4,2,1,3,0:T(8,128)(2,1)}, u32[]{:S(2)}, u32[]{:S(2)}) %all-to-all-start.6) | async-done | bytes 1572896 | tf_op jit(solution)/shard_map/all_to_all | solution.py:108
  439.9 1.6 bitcast_convert_fusion
  441.6 1.8 gather_fusion.7
  443.4 1.6 bitcast_select_fusion.2
  445.1 1.3 fusion.56
  446.4 0.3 multiply_reduce_fusion
  446.7 2.8 convolution_convert_fusion.2
  449.5 90.4 %reduce-scatter.5.cloned.1.call-done = bf16[96,1024]{1,0:T(8,128)(2,1)} async-done(((bf16[768,1024]{1,0:T(8,128)(2,1)}), bf16[96,1024]{1,0:T(8,128)(2,1)}) %reduce-scatter.5.cloned.1.call-update) | async-done | bytes 196624 | tf_op jit(solution)/shard_map/reduce_scatter | solution.py:131
  539.9 1.7 add_convert_fusion
  (70 shorter events, 3.1 us)
Async XLA Ops:
  8.8 12.9 %copy-start.5 = (s32[16,4]{0,1:T(4,128)S(1)}, s32[16,4]{0,1:T(4,128)}, u32[]{:S(2)}) copy-start(s32[16,4]{0,1:T(4,128)} %param.18) | copy-start | bytes 772
  8.8 13.1 %copy-start.4 = (s32[16]{0:T(128)S(1)}, s32[16]{0:T(128)}, u32[]{:S(2)}) copy-start(s32[16]{0:T(128)} %param.19) | copy-start | bytes 196
  8.8 38.3 %all-to-all-start.1 = ((bf16[8,96,1024]{2,1,0:T(8,128)(2,1)}), bf16[8,96,1024]{2,1,0:T(8,128)(2,1)S(1)}, u32[]{:S(2)}, u32[]{:S(2)}) async-start(bf16[8,96,1024]{2,1,0:T(8,128)(2,1)} %stack.13), calls=%async_computation.1 | async-start | bytes 3145728 | tf_op jit(solution)/shard_map/all_to_all | solution.py:65
  47.1 35.8 %all-to-all-start = ((s32[64,2,3]{2,1,0:T(2,128)}), s32[64,2,3]{2,1,0:T(2,128)S(1)}, u32[]{:S(2)}, u32[]{:S(2)}) async-start(s32[64,2,3]{2,1,0:T(2,128)} %copy.62), calls=%async_computation | async-start | bytes 131072 | tf_op jit(solution)/shard_map/all_to_all | solution.py:83
  74.6 1.6 copy-start.6
  83.0 47.9 %all-to-all-start.2 = ((bf16[64,2,48,1,128]{4,2,1,3,0:T(8,128)(2,1)}), bf16[64,2,48,1,128]{4,2,1,3,0:T(8,128)(2,1)}, u32[]{:S(2)}, u32[]{:S(2)}) async-start(bf16[64,2,48,1,128]{4,2,1,3,0:T(8,128)(2,1)} %bitcast.39), calls=%async_computation.2 | async-start | bytes 3145728 | tf_op jit(solution)/shard_map/all_to_all | solution.py:82
  134.9 45.9 %all-to-all-start.3 = ((bf16[64,2,48,1,128]{4,2,1,3,0:T(8,128)(2,1)}), bf16[64,2,48,1,128]{4,2,1,3,0:T(8,128)(2,1)}, u32[]{:S(2)}, u32[]{:S(2)}) async-start(bf16[64,2,48,1,128]{4,2,1,3,0:T(8,128)(2,1)} %fusion.12), calls=%async_computation.3 | async-start | bytes 3145728 | tf_op jit(solution)/shard_map/all_to_all | solution.py:108
  141.7 145.3 %reduce-scatter.3.cloned.1.call-start = ((), (), s32[]{:S(2)}) async-start(), calls=%async_computation.9 | async-start | bytes 1769472 | tf_op jit(solution)/shard_map/reduce_scatter | solution.py:131
  192.1 1.0 copy-start.2
  193.2 93.8 %copy-start = (bf16[96,1024]{1,0:T(8,128)(2,1)S(1)}, bf16[96,1024]{1,0:T(8,128)(2,1)}, u32[]{:S(2)}) copy-start(bf16[96,1024]{1,0:T(8,128)(2,1)} %param.14) | copy-start | bytes 589828
  315.9 1.6 copy-start.7
  319.8 81.1 %copy-start.1 = (bf16[768,1,512]{2,0,1:T(8,128)(2,1)}, bf16[768,1,512]{2,0,1:T(8,128)(2,1)S(1)}, u32[]{:S(2)}) copy-start(bf16[768,1,512]{2,0,1:T(8,128)(2,1)S(1)} %get-tuple-element.47) | copy-start | bytes 2359300
  324.6 65.5 %all-to-all-start.5 = ((bf16[64,2,48,1,128]{4,2,1,3,0:T(8,128)(2,1)}), bf16[64,2,48,1,128]{4,2,1,3,0:T(8,128)(2,1)}, u32[]{:S(2)}, u32[]{:S(2)}) async-start(bf16[64,2,48,1,128]{4,2,1,3,0:T(8,128)(2,1)} %bitcast.195), calls=%async_computation.6 | async-start | bytes 3145728 | tf_op jit(solution)/shard_map/all_to_all | solution.py:82
  394.1 45.9 %all-to-all-start.6 = ((bf16[64,2,48,1,128]{4,2,1,3,0:T(8,128)(2,1)}), bf16[64,2,48,1,128]{4,2,1,3,0:T(8,128)(2,1)}, u32[]{:S(2)}, u32[]{:S(2)}) async-start(bf16[64,2,48,1,128]{4,2,1,3,0:T(8,128)(2,1)} %fusion.13), calls=%async_computation.7 | async-start | bytes 3145728 | tf_op jit(solution)/shard_map/all_to_all | solution.py:108
  400.8 139.1 %reduce-scatter.5.cloned.1.call-start = ((), (), s32[]{:S(2)}) async-start(), calls=%async_computation.10 | async-start | bytes 1769472 | tf_op jit(solution)/shard_map/reduce_scatter | solution.py:131
  445.0 1.7 copy-start.3
Sparse Core Ops, SparseCore 0:
  196.1 90.8 reduce-scatter.2
  449.6 90.2 reduce-scatter.4
